TPU v7x, 256 devices: a whole 4x4x8 slice. The times are simulated.
256 devices in a mesh: row: 4 (over z_hi, core), real: 64 (over x, y, z_lo).
Axes of the slice: x: 4, y: 4, z: 8 (z_hi: 2, z_lo: 4; z = z_hi * 4 + z_lo), core: 2. Of those that a mesh axis runs over, the one named last changes fastest.
Arguments:
- right_sides: float32 [10, 4, 256, 32768], P(None, 'row', None, 'real'), may hold values from -8 to 8
- factor: float32 [10, 4, 256, 1024], P(None, 'row', None, 'real'), may hold values from -1 to 2, as said below
Outputs:
- updated: float32 [10, 4, 256, 32768], P(None, 'row', None, 'real')
Inputs may be any that keep to these rules, and one draw needn't show every extreme that they name: factor is lower triangular in global row and column order (entries with column above the global row are 0), with diagonal entries from 1 to 2.
All inputs are finite; a program needn't handle non-finite values.
Results may differ from a plain program's by a relative error of at most 0.0001.
Values sent between devices are 32-bit elements; how exact they have to be, the bound alone decides.
A program may use at most 128 MiB of HBM per device.

v0:
```python
import jax
import jax.numpy as jnp
from jax import lax
from jax.sharding import PartitionSpec as P


def broadcast(value, axis, source):
    kept = jnp.where(lax.axis_index(axis) == source, value, 0).astype(value.dtype)
    return lax.psum(kept, axis)


def forward_chain(head_rows, current, position, row_count):
    span_cols = current.shape[0]
    solved = []
    for panel_index in range(row_count):
        columns = head_rows[:, panel_index * span_cols : (panel_index + 1) * span_cols]
        candidate = lax.linalg.triangular_solve(columns, current, left_side=True, lower=True)
        answer = broadcast(candidate, "row", panel_index)
        update = jnp.dot(columns, answer, precision=lax.Precision.HIGHEST)
        current = jnp.where(
            position > panel_index,
            current - update,
            jnp.where(position == panel_index, answer, current),
        )
        solved.append(answer)
    return (current, jnp.concatenate(solved, axis=0))


def body(right_sides, factor):
    position = lax.axis_index("row")
    row_count = lax.axis_size("row")
    working = right_sides[:, 0]
    gathered = lax.all_gather(factor, "real", axis=3, tiled=True)[:, 0]
    head_rows = gathered[0]
    first, window_solved = forward_chain(head_rows, working[0], position, row_count)
    trailing = working[1:] - jnp.einsum(
        "bpw,wc->bpc", gathered[1:], window_solved, precision=lax.Precision.HIGHEST
    )
    return jnp.concatenate([first[None], trailing], axis=0)[:, None]


def solution(mesh):
    placed = (P(None, "row", None, "real"), P(None, "row", None, "real"))
    return jax.shard_map(
        body, mesh=mesh, in_specs=placed, out_specs=P(None, "row", None, "real"), check_vma=False
    )
```

profile of v0, /device:TPU:2, one launch (start us, length us, event | category | flops | bytes accessed | tf_op | source)
XLA Modules:
  0.0 707.7 jit_solution(12158152810625708510)
XLA Ops:
  6.5 1.7 copy.12
  8.4 1.1 slice_bitcast_fusion
  9.5 350.4 %all-gather.2.cloned.1.call-done = f32[10,1,256,1024]{2,1,0,3:T(1,128)} async-done(((f32[10,1,256,16]{2,1,0,3:T(1,128)}), f32[10,1,256,1024]{2,1,0,3:T(1,128)}) %all-gather.2.cloned.1.call-update) | async-done | bytes 10485776 | tf_op jit(solution)/shard_map/all_gather | solution.py:33
  359.9 1.9 slice.109
  362.1 4.1 while.8
  362.1 0.6 fusion.64
  362.7 1.3 dynamic-slice.22
  364.1 0.6 fusion.64
  364.7 1.3 dynamic-slice.22
  366.1 19.7 %custom-call.6 = f32[2,128,128]{1,2,0:T(8,128)S(1)} custom-call(f32[2,128,128]{2,1,0:T(8,128)S(1)} %get-tuple-element.32), custom_call_target="InvertDiagBlocksLowerTriangular" | custom-call | tf_op jit(solution)/shard_map/triangular_solve/custom-call.1 | solution.py:17
  387.1 0.8 maximum_select_fusion
  388.0 4.1 while.9
  388.0 0.6 fusion.65
  388.7 1.3 dynamic-slice.24
  390.1 0.6 fusion.65
  390.7 1.3 dynamic-slice.24
  392.1 19.7 %custom-call.7 = f32[2,128,128]{1,2,0:T(8,128)S(1)} custom-call(f32[2,128,128]{2,1,0:T(8,128)S(1)} %get-tuple-element.33), custom_call_target="InvertDiagBlocksLowerTriangular" | custom-call | tf_op jit(solution)/shard_map/triangular_solve/custom-call.1 | solution.py:17
  411.8 64.5 %all-reduce.5.cloned.1.call-done = f32[256,512]{1,0:T(8,128)} async-done(((f32[256,512]{1,0:T(8,128)}), f32[256,512]{1,0:T(8,128)}) %all-reduce.5.cloned.1.call-update) | async-done | bytes 524304 | tf_op jit(solution)/shard_map/psum | solution.py:9
  476.3 2.2 fusion.11
  479.7 0.8 maximum_select_fusion.1
  480.8 4.2 while.10
  480.9 0.6 fusion.66
  481.5 1.3 dynamic-slice.26
  483.0 0.6 fusion.66
  483.6 1.3 dynamic-slice.26
  485.0 19.7 %custom-call.8 = f32[2,128,128]{1,2,0:T(8,128)S(1)} custom-call(f32[2,128,128]{2,1,0:T(8,128)S(1)} %get-tuple-element.34), custom_call_target="InvertDiagBlocksLowerTriangular" | custom-call | tf_op jit(solution)/shard_map/triangular_solve/custom-call.1 | solution.py:17
  504.7 31.5 %all-reduce.7.cloned.1.call-done = f32[256,512]{1,0:T(8,128)} async-done(((f32[256,512]{1,0:T(8,128)}), f32[256,512]{1,0:T(8,128)}) %all-reduce.7.cloned.1.call-update) | async-done | bytes 524304 | tf_op jit(solution)/shard_map/psum | solution.py:9
  536.2 1.9 fusion.13
  539.4 0.8 maximum_select_fusion.2
  540.3 4.4 while.11
  540.4 0.7 fusion.67
  541.0 1.4 dynamic-slice.28
  542.6 0.7 fusion.67
  543.2 1.4 dynamic-slice.28
  544.8 19.7 %custom-call.9 = f32[2,128,128]{1,2,0:T(8,128)S(1)} custom-call(f32[2,128,128]{2,1,0:T(8,128)S(1)} %get-tuple-element.35), custom_call_target="InvertDiagBlocksLowerTriangular" | custom-call | tf_op jit(solution)/shard_map/triangular_solve/custom-call.1 | solution.py:17
  564.4 31.4 %all-reduce.9.cloned.1.call-done = f32[256,512]{1,0:T(8,128)} async-done(((f32[256,512]{1,0:T(8,128)}), f32[256,512]{1,0:T(8,128)}) %all-reduce.9.cloned.1.call-update) | async-done | bytes 524304 | tf_op jit(solution)/shard_map/psum | solution.py:9
  595.9 1.9 fusion.15
  599.1 0.9 maximum_select_fusion.3
  600.0 5.0 slice.53
  605.0 6.1 copy.37
  611.1 8.9 %slice.134 = f32[9,1,256,1024]{2,1,0,3:T(1,128)} slice(f32[10,1,256,1024]{2,1,0,3:T(1,128)} %all-gather.2.cloned.1.call-done), slice={[1:10], [0:1], [0:256], [0:1024]} | slice | bytes 18874368 | tf_op jit(solution)/shard_map/slice | solution.py:37
  620.0 21.8 %copy.38 = f32[9,1,256,1024]{3,2,0,1:T(8,128)} copy(f32[9,1,256,1024]{2,1,0,3:T(1,128)} %slice.134) | data formatting | bytes 18874368
  641.8 13.9 %all-reduce.11.cloned.1.call-done = f32[256,512]{1,0:T(8,128)} async-done(((f32[256,512]{1,0:T(8,128)}), f32[256,512]{1,0:T(8,128)}) %all-reduce.11.cloned.1.call-update) | async-done | bytes 524304 | tf_op jit(solution)/shard_map/psum | solution.py:9
  655.7 2.7 fusion.18
  658.4 1.2 copy.24
  659.7 32.6 %bitcast_subtract_fusion = f32[9,256,512]{1,2,0:T(8,128)S(1)} fusion(f32[9,1,256,512]{2,3,0,1:T(8,128)} %copy.37, f32[9,1,256,1024]{3,2,0,1:T(8,128)} %copy.38, f32[256,512]{1,0:T(8,128)} %all-reduce.11.cloned.1.call-done, f32[256,512]{1,0:T(8,128)S(1)} %copy-done.2, f32[256,512]{1,0:T(8,128)S(1)} %copy-done.1, f32[256,512]{1,0:T(8,128)S(1)} %copy-done), kind=kOutput, calls=%fused_computation.11 | convolution fusion | flops 14498267136 | bytes 20971520 | tf_op jit(solution)/shard_map/bpw,wc->bpc/dot_general | solution.py:36
  692.3 2.9 maximum_bitcast_fusion
  695.3 5.9 copy.25
  (60 shorter events, 6.6 us)
Async XLA Ops:
  6.5 353.3 %all-gather.2.cloned.1.call-start = ((), (), s32[]{:S(2)}) async-start(), calls=%async_computation | async-start | bytes 10649600 | tf_op jit(solution)/shard_map/all_gather | solution.py:33
  8.3 468.0 %all-reduce.5.cloned.1.call-start = ((), (), s32[]{:S(2)}) async-start(), calls=%async_computation.1 | async-start | bytes 1048576 | tf_op jit(solution)/shard_map/psum | solution.py:9
  388.0 148.3 %all-reduce.7.cloned.1.call-start = ((), (), s32[]{:S(2)}) async-start(), calls=%async_computation.2 | async-start | bytes 1048576 | tf_op jit(solution)/shard_map/psum | solution.py:9
  480.6 115.3 %all-reduce.9.cloned.1.call-start = ((), (), s32[]{:S(2)}) async-start(), calls=%async_computation.3 | async-start | bytes 1048576 | tf_op jit(solution)/shard_map/psum | solution.py:9
  540.3 115.4 %all-reduce.11.cloned.1.call-start = ((), (), s32[]{:S(2)}) async-start(), calls=%async_computation.4 | async-start | bytes 1048576 | tf_op jit(solution)/shard_map/psum | solution.py:9
  619.9 39.7 %copy-start = (f32[256,512]{1,0:T(8,128)S(1)}, f32[256,512]{1,0:T(8,128)}, u32[]{:S(2)}) copy-start(f32[256,512]{1,0:T(8,128)} %all-reduce.5.cloned.1.call-done) | copy-start | bytes 1572868
  619.9 39.7 %copy-start.1 = (f32[256,512]{1,0:T(8,128)S(1)}, f32[256,512]{1,0:T(8,128)}, u32[]{:S(2)}) copy-start(f32[256,512]{1,0:T(8,128)} %all-reduce.7.cloned.1.call-done) | copy-start | bytes 1572868
  620.0 39.7 %copy-start.2 = (f32[256,512]{1,0:T(8,128)S(1)}, f32[256,512]{1,0:T(8,128)}, u32[]{:S(2)}) copy-start(f32[256,512]{1,0:T(8,128)} %all-reduce.9.cloned.1.call-done) | copy-start | bytes 1572868
Sparse Core Ops, SparseCore 0:
  9.1 350.6 all-gather.1
  388.1 88.1 all-reduce.4
  480.7 55.4 all-reduce.6
  540.4 55.4 all-reduce.8
  600.1 55.5 all-reduce.10
where the time goes:
time: 710 us; the launch traced here: 708 us
  waiting for transfers between devices  492 us (69%)
  other arithmetic  85.1 us (12%)
  local copies, waits for them, and re-layouts  70.3 us (10%)
  matrix products  46.4 us (7%)
  between operations  13.5 us (2%)
    all_gather x1, waiting for transfers between devices, body(): gathered = lax.all_gather(factor, 'real', axis=3, tiled=True)[:, 0]  350 us
    psum x4, waiting for transfers between devices, broadcast(): return lax.psum(kept, axis)  141 us
    another operation x6, other arithmetic, forward_chain(): lax.linalg.triangular_solve(columns, current, left_side=True, lower=True)  78.8 us
    dot_general x1, matrix products, body(): jnp.einsum('bpw,wc->bpc', gathered[1:], window_solved, precision=lax.Prec...  32.6 us
    unnamed x10, local copies, waits for them, and re-layouts  29.7 us
    another operation x44, local copies, waits for them, and re-layouts, forward_chain(): lax.linalg.triangular_solve(columns, current, left_side=True, lower=True)  16.5 us
  transfers between devices with their start and end apart: 5, of which 5 were waited for; matrix products, arithmetic and copies ran while one was open for 16% of the time, Pallas kernels for 0%

commit v1 on v0

v1 whole, which is shorter than its diff:
```python
import jax
import jax.numpy as jnp
from jax import lax
from jax.experimental import pallas as pl
from jax.experimental.pallas import tpu as pltpu
from jax.sharding import PartitionSpec as P

MESH = pl.DeviceIdType.MESH
PIECES = 11
SLOTS = 13
HI = lax.Precision.HIGHEST


def gather_kernel(ft, rhs, lt, bh, rsem, zsem, zsend, ssem, bsem, bsend, xsem, xsend):
    row = lax.axis_index("row")
    real = lax.axis_index("real")
    zh, core = row // 2, row % 2
    x0, y0, z0 = real // 16, (real // 4) % 4, real % 4
    other = (1 - zh) * 2 + core
    sibling = zh * 2 + (1 - core)

    def place(x, y, z):
        return (x % 4) * 16 + (y % 4) * 4 + z

    near = [(row, place(x0 + d, y0, z0)) for d in (1, 3)]
    near += [(row, place(x0, y0 + d, z0)) for d in (1, 3)]
    near += [(row, place(x0, y0, (z0 + d) % 4)) for d in (1, 2, 3)]
    near += [(other, place(x0, y0, z)) for z in range(4)]
    near += [(sibling, real)]
    barrier = pltpu.get_barrier_semaphore()
    for device in near:
        pl.semaphore_signal(barrier, inc=1, device_id=device, device_id_type=MESH)
    pl.semaphore_wait(barrier, len(near))

    def chunk(p, h):
        return lt.at[p, h, x0 * 4 + y0, pl.ds(16 * z0, 16)]

    def own(block, h):
        return ft.at[block, :, pl.ds(128 * h, 128)]

    def scatter_z(p, block):
        for h in (0, 1):
            pltpu.make_async_copy(own(block, h), chunk(p, h), zsem.at[p, h]).start()
            for d in (1, 2, 3):
                pltpu.make_async_remote_copy(
                    own(block, h), chunk(p, h), zsend.at[p, h], zsem.at[p, h],
                    device_id=(row, place(x0, y0, (z0 + d) % 4)), device_id_type=MESH,
                ).start()

    scatter_z(0, 0)
    for h in (0, 1):
        for z in range(4):
            pltpu.make_async_remote_copy(
                own(0, h), chunk(1, h), zsend.at[1, h], zsem.at[1, h],
                device_id=(other, place(x0, y0, z)), device_id_type=MESH,
            ).start()
    half_copy = pltpu.make_async_remote_copy(
        rhs.at[0], bh.at[0], bsend.at[0], bsem.at[0], device_id=(other, real), device_id_type=MESH
    )
    half_copy.start()
    core_copy = pltpu.make_async_remote_copy(
        rhs.at[0], bh.at[1], bsend.at[1], bsem.at[1], device_id=(sibling, real), device_id_type=MESH
    )
    core_copy.start()

    @pl.loop(2, PIECES)
    def _(p):
        scatter_z(p, p - 1)

    def slab(p, h, a, b, half=None):
        x, y = ((x0 + a) % 4, (y0 + b) % 4) if h == 0 else ((x0 + b) % 4, (y0 + a) % 4)
        if half is None:
            return lt.at[p, h, x * 4 + y]
        return lt.at[p, h, x * 4 + y, pl.ds(32 * half, 32)]

    def target(h, first, step):
        if (h == 0) == first:
            return (row, place(x0 + step, y0, z0))
        return (row, place(x0, y0 + step, z0))

    def send(p, h, a, b, first, step, k, half=None):
        ref = slab(p, h, a, b, half)
        pltpu.make_async_remote_copy(
            ref, ref, ssem.at[p, h], rsem.at[p, h, k],
            device_id=target(h, first, step), device_id_type=MESH,
        ).start()

    def await_rows(p, h, k, slabs=1):
        ref = lt.at[p, h, pl.ds(0, slabs)]
        pltpu.make_async_copy(ref, ref, rsem.at[p, h, k]).wait()

    def phase1(p):
        for h in (0, 1):
            ref = lt.at[p, h, 0]
            pltpu.make_async_copy(ref, ref, zsem.at[p, h]).wait()
            send(p, h, 0, 0, True, 1, 1)
            send(p, h, 0, 0, True, 3, 2)
            send(p, h, 0, 0, False, 1, 4)
            send(p, h, 0, 0, False, 3, 5)

    def phase2(p):
        for h in (0, 1):
            await_rows(p, h, 1)
            send(p, h, 3, 0, True, 1, 3, 0)
            send(p, h, 3, 0, False, 1, 7)
            send(p, h, 3, 0, False, 3, 8)
        for h in (0, 1):
            await_rows(p, h, 2)
            send(p, h, 1, 0, True, 3, 3, 1)
            send(p, h, 1, 0, False, 1, 7)
            send(p, h, 1, 0, False, 3, 8)
        for h in (0, 1):
            await_rows(p, h, 4)
            send(p, h, 0, 3, False, 1, 6, 0)
            await_rows(p, h, 5)
            send(p, h, 0, 1, False, 3, 6, 1)

    def phase3(p):
        for h in (0, 1):
            await_rows(p, h, 3)
            send(p, h, 2, 0, False, 1, 10)
            send(p, h, 2, 0, False, 3, 11)
        for h in (0, 1):
            await_rows(p, h, 7, 2)
            send(p, h, 3, 3, False, 1, 9, 0)
            send(p, h, 1, 3, False, 1, 9, 0)
            await_rows(p, h, 8, 2)
            send(p, h, 3, 1, False, 3, 9, 1)
            send(p, h, 1, 1, False, 3, 9, 1)

    def phase4(p):
        for h in (0, 1):
            await_rows(p, h, 10)
            send(p, h, 2, 3, False, 1, 12, 0)
            await_rows(p, h, 11)
            send(p, h, 2, 1, False, 3, 12, 1)

    def finish(p):
        for h in (0, 1):
            await_rows(p, h, 6)
            await_rows(p, h, 9, 2)
            await_rows(p, h, 12)

    @pl.loop(0, PIECES + 5)
    def _(t):
        pl.when(t < PIECES)(lambda: phase1(t))
        pl.when((t >= 2) & (t < PIECES + 2))(lambda: phase2(t - 2))
        pl.when((t >= 3) & (t < PIECES + 3))(lambda: phase3(t - 3))
        pl.when((t >= 4) & (t < PIECES + 4))(lambda: phase4(t - 4))
        pl.when(t >= 5)(lambda: finish(t - 5))

        @pl.when(t == 6)
        def _():
            for p in (0, 1):
                pltpu.make_async_remote_copy(
                    lt.at[p], lt.at[PIECES + p], xsend.at[p], xsem.at[p],
                    device_id=(sibling, real), device_id_type=MESH,
                ).start()

    half_copy.wait()
    core_copy.wait()
    last = pltpu.make_async_remote_copy(
        bh.at[0], bh.at[2], bsend.at[2], bsem.at[2], device_id=(sibling, real), device_id_type=MESH
    )
    last.start()
    last.wait()
    for p in (0, 1):
        pltpu.make_async_remote_copy(
            lt.at[p], lt.at[PIECES + p], xsend.at[p], xsem.at[p],
            device_id=(sibling, real), device_id_type=MESH,
        ).wait()

    @pl.loop(0, PIECES)
    def _(p):
        for h in (0, 1):
            part = lt.at[p, h, 0, pl.ds(0, 48)]
            pltpu.make_async_copy(part, part, zsend.at[p, h]).wait()
            part = lt.at[p, h, pl.ds(0, 15)]
            pltpu.make_async_copy(part, part, ssem.at[p, h]).wait()

    for h in (0, 1):
        part = lt.at[1, h, 0, pl.ds(0, 16)]
        pltpu.make_async_copy(part, part, zsend.at[1, h]).wait()


def gather(ft, rhs):
    dma = pltpu.SemaphoreType.DMA
    anywhere = pl.BlockSpec(memory_space=pl.ANY)
    return pl.pallas_call(
        gather_kernel,
        out_shape=(
            jax.ShapeDtypeStruct((SLOTS, 2, 16, 64, 128), jnp.float32),
            jax.ShapeDtypeStruct((3, 256, 512), jnp.float32),
        ),
        in_specs=[anywhere, anywhere],
        out_specs=(anywhere, anywhere),
        scratch_shapes=[
            dma((PIECES, 2, 13)), dma((PIECES, 2)), dma((PIECES, 2)), dma((PIECES, 2)),
            dma((3,)), dma((3,)), dma((2,)), dma((2,)),
        ],
        compiler_params=pltpu.CompilerParams(collective_id=0, has_side_effects=True),
        name="gather",
    )(ft, rhs)


def dot_t(a, b, precision=None):
    return lax.dot_general(
        a, b, (((0,), (0,)), ((), ())), precision=precision, preferred_element_type=jnp.float32
    )


def split(value):
    high = value.astype(jnp.bfloat16)
    return high, (value - high.astype(jnp.float32)).astype(jnp.bfloat16)


def invert(upper):
    r = lax.broadcasted_iota(jnp.int32, (128, 128), 0)
    c = lax.broadcasted_iota(jnp.int32, (128, 128), 1)
    diagonal = jnp.where(r == c, upper, 0.0)
    x = jnp.where(r == c, 1.0 / jnp.sum(diagonal, axis=0, keepdims=True), 0.0)
    size = 1
    while size < 128:
        cross = jnp.where((c // (2 * size) == r // (2 * size)) & (c // size != r // size) & (c > r), upper, 0.0)
        inner = jnp.dot(x, cross, precision=HI, preferred_element_type=jnp.float32)
        x = x - jnp.dot(inner, x, precision=HI, preferred_element_type=jnp.float32)
        size *= 2
    return x


def solve_kernel(rhs, lt, lt_all, bh, out, head, first, sem, y, yh, yl):
    b = pl.program_id(0)
    row = lax.axis_index("row")
    zh, core = row // 2, row % 2

    @pl.when(b == 0)
    def _():
        copies = []
        for k in range(4):
            kh, kc = k // 2, k % 2
            away = (kh + zh) % 2
            side = (kc + core) % 2
            slot = away + 11 * side
            copies.append(pltpu.make_async_copy(lt_all.at[slot], head.at[k], sem.at[k]))
        for i in range(3):
            copies.append(pltpu.make_async_copy(bh.at[i], first.at[i], sem.at[4 + i]))
        for copy in copies:
            copy.start()
        first[3] = rhs[0]
        for copy in copies:
            copy.wait()
        for k in range(4):
            kh, kc = k // 2, k % 2
            away = (kh + zh) % 2
            side = (kc + core) % 2
            index = jnp.where(away == 1, jnp.where(side == 1, 2, 0), jnp.where(side == 1, 1, 3))
            for h in (0, 1):
                at = 256 * k + 128 * h
                value = first[index, pl.ds(128 * h, 128), :]
                if at:
                    value = value - dot_t(head[k, h, 0:at, :], y[0:at, :], HI)
                x = invert(head[k, h, at : at + 128, :])
                y[at : at + 128, :] = dot_t(x, value, HI)
        high, low = split(y[...])
        yh[...] = high
        yl[...] = low
        out[0] = y[pl.ds(pl.multiple_of(row * 256, 256), 256), :]

    @pl.when(b > 0)
    def _():
        for h in (0, 1):
            high, low = split(lt[0, h])
            update = dot_t(high, yh[...]) + dot_t(high, yl[...]) + dot_t(low, yh[...])
            out[0, 128 * h : 128 * h + 128, :] = rhs[0, 128 * h : 128 * h + 128, :] - update


def solve(rhs, lt, bh):
    anywhere = pl.BlockSpec(memory_space=pl.ANY)
    return pl.pallas_call(
        solve_kernel,
        out_shape=jax.ShapeDtypeStruct((10, 256, 512), jnp.float32),
        grid=(10,),
        in_specs=[
            pl.BlockSpec((1, 256, 512), lambda b: (b, 0, 0)),
            pl.BlockSpec((1, 2, 1024, 128), lambda b: (jnp.maximum(b, 1) + 1, 0, 0, 0)),
            anywhere,
            anywhere,
        ],
        out_specs=pl.BlockSpec((1, 256, 512), lambda b: (b, 0, 0)),
        scratch_shapes=[
            pltpu.VMEM((4, 2, 1024, 128), jnp.float32),
            pltpu.VMEM((4, 256, 512), jnp.float32),
            pltpu.SemaphoreType.DMA((7,)),
            pltpu.VMEM((1024, 512), jnp.float32),
            pltpu.VMEM((1024, 512), jnp.bfloat16),
            pltpu.VMEM((1024, 512), jnp.bfloat16),
        ],
        compiler_params=pltpu.CompilerParams(vmem_limit_bytes=60 * 1024 * 1024),
        name="solve",
    )(rhs, lt, lt, bh)


def body(right_sides, factor):
    rhs = right_sides[:, 0]
    lt, bh = gather(jnp.swapaxes(factor[:, 0], 1, 2), rhs)
    return solve(rhs, lt.reshape(SLOTS, 2, 1024, 128), bh)[:, None]


def solution(mesh):
    placed = (P(None, "row", None, "real"), P(None, "row", None, "real"))
    return jax.shard_map(
        body, mesh=mesh, in_specs=placed, out_specs=P(None, "row", None, "real"), check_vma=False
    )
```

time: 710 us -> 153 us (0.22)
  waiting for transfers between devices: 492 us -> 0 us
  Pallas kernels: 0 us -> 151 us
  other arithmetic: 85.1 us -> 0 us
  local copies, waits for them, and re-layouts: 70.3 us -> 0 us
  matrix products: 46.4 us -> 0 us
  between operations: 13.5 us -> 0.01 us
    all_gather x1 -> x0, waiting for transfers between devices: 350 us -> none  [body(): gathered = lax.all_gather(factor, 'real', axis=3, tiled=True)[:, 0]]
    pallas_call x0 -> x2, Pallas kernels: none -> 151 us  [the longest x1 105 us: gather(): pl.pallas_call(gather_kernel, out_shape=(jax.ShapeDtypeStruct((SLOTS, 2,...]
    psum x4 -> x0, waiting for transfers between devices: 141 us -> none  [broadcast(): return lax.psum(kept, axis)]
    another operation x6 -> x0, other arithmetic: 78.8 us -> none  [forward_chain(): lax.linalg.triangular_solve(columns, current, left_side=True, lower=True)]
    dot_general x5 -> x0, matrix products: 41.3 us -> none  [the longest x1 32.6 us: body(): jnp.einsum('bpw,wc->bpc', gathered[1:], window_solved, precision=lax.Prec...]
    unnamed x10 -> x0, local copies, waits for them, and re-layouts: 29.7 us -> none
    another operation x44 -> x0, local copies, waits for them, and re-layouts: 16.5 us -> none  [forward_chain(): lax.linalg.triangular_solve(columns, current, left_side=True, lower=True)]
    slice x3 -> x0, local copies, waits for them, and re-layouts: 15.8 us -> none  [the longest x1 8.87 us: body(): gathered[1:]]
  transfers between devices with their start and end apart: 5 -> 0, of which waited for: 5 -> 0; matrix products, arithmetic and copies ran while one was open for 16% -> 0% of each run, Pallas kernels for 0% -> 0%
where the time goes in v1:
time: 153 us; the launch traced here: 151 us
  Pallas kernels  151 us (99%)
    pallas_call x1, Pallas kernels, gather(): pl.pallas_call(gather_kernel, out_shape=(jax.ShapeDtypeStruct((SLOTS, 2,...  105 us
    pallas_call x1, Pallas kernels, solve(): pl.pallas_call(solve_kernel, out_shape=jax.ShapeDtypeStruct((10, 256, 512...  46.6 us

profile of v1, /device:TPU:2, one launch (start us, length us, event | category | flops | bytes accessed | tf_op | source)
XLA Modules:
  0.0 151.2 jit_solution(14118979113073627225)
XLA Ops:
  0.0 104.6 %gather.1 = (f32[13,2,16,64,128]{4,3,2,1,0:T(8,128)}, f32[3,256,512]{2,1,0:T(8,128)}) custom-call(f32[10,16,256]{2,1,0:T(8,128)} %bitcast.12, f32[10,256,512]{2,1,0:T(8,128)} %bitcast.10), custom_call_target="tpu_custom_call" | custom-call | tf_op jit(solution)/shard_map/gather/pallas_call | solution.py:189
  104.6 46.6 %solve.1 = f32[10,256,512]{2,1,0:T(8,128)} custom-call(f32[10,256,512]{2,1,0:T(8,128)} %bitcast.11, f32[13,2,1024,128]{3,2,1,0:T(8,128)} %bitcast.8, f32[13,2,1024,128]{3,2,1,0:T(8,128)} %bitcast.9, f32[3,256,512]{2,1,0:T(8,128)} %get-tuple-element.8.bh), custom_call_target="tpu_custom_call" | custom-call | tf_op jit(solution)/shard_map/solve/pallas_call | solution.py:279

commit v2 on v0

v2 whole, which is shorter than its diff:
```python
import jax
import jax.numpy as jnp
from jax import lax
from jax.experimental import pallas as pl
from jax.experimental.pallas import tpu as pltpu
from jax.sharding import PartitionSpec as P

MESH = pl.DeviceIdType.MESH
PIECES = 11
SLOTS = 13
AHEAD = 4
RIGHT_FROM, RIGHT_BY = 4, 9
INVERT_OWN, INVERT_SIBLING, SOLVE = 7, 8, 10
HI = lax.Precision.HIGHEST


def dot(a, b, precision=None):
    return jnp.dot(a, b, precision=precision, preferred_element_type=jnp.float32)


def dot_t(a, b, precision=None):
    return lax.dot_general(
        a, b, (((0,), (0,)), ((), ())), precision=precision, preferred_element_type=jnp.float32
    )


def split(value):
    high = value.astype(jnp.bfloat16)
    return high, (value - high.astype(jnp.float32)).astype(jnp.bfloat16)


def product(lt_part, yh, yl):
    high, low = split(lt_part)
    return dot_t(high, yh) + dot_t(high, yl) + dot_t(low, yh)


def invert(uppers):
    r = lax.broadcasted_iota(jnp.int32, (128, 128), 0)
    c = lax.broadcasted_iota(jnp.int32, (128, 128), 1)
    xs = [
        jnp.where(r == c, 1.0 / jnp.sum(jnp.where(r == c, u, 0.0), axis=0, keepdims=True), 0.0)
        for u in uppers
    ]
    size = 1
    while size < 128:
        cross = (c // (2 * size) == r // (2 * size)) & (c // size != r // size) & (c > r)
        inner = [dot(x, jnp.where(cross, u, 0.0), HI) for x, u in zip(xs, uppers)]
        xs = [x - dot(i, x, HI) for x, i in zip(xs, inner)]
        size *= 2
    return xs


def kernel(
    ft, rhs, out, lt, stage, bh, work, xinv, y, yh, yl,
    rsem, zsem, zsend, ssem, stsem, bsem, bsend, xsem, xsend, insem, outsem,
):
    row = lax.axis_index("row")
    real = lax.axis_index("real")
    zh, core = row // 2, row % 2
    x0, y0, z0 = real // 16, (real // 4) % 4, real % 4
    other = (1 - zh) * 2 + core
    sibling = zh * 2 + (1 - core)

    def place(x, y, z):
        return (x % 4) * 16 + (y % 4) * 4 + z

    near = [(row, place(x0 + d, y0, z0)) for d in (1, 3)]
    near += [(row, place(x0, y0 + d, z0)) for d in (1, 3)]
    near += [(row, place(x0, y0, (z0 + d) % 4)) for d in (1, 2, 3)]
    near += [(other, place(x0, y0, z)) for z in range(4)]
    near += [(sibling, real)]
    barrier = pltpu.get_barrier_semaphore()
    pltpu.make_async_copy(rhs, work, insem.at[0]).start()
    pltpu.make_async_copy(rhs.at[0], bh.at[3], insem.at[1]).start()
    for h in (0, 1):
        pltpu.make_async_copy(ft.at[:, :, pl.ds(128 * h, 128)], stage.at[:, h], stsem.at[h]).start()
    for device in near:
        pl.semaphore_signal(barrier, inc=1, device_id=device, device_id_type=MESH)
    for h in (0, 1):
        pltpu.make_async_copy(ft.at[:, :, pl.ds(128 * h, 128)], stage.at[:, h], stsem.at[h]).wait()
    pl.semaphore_wait(barrier, len(near))

    def chunk(p):
        return lt.at[p, :, x0 * 4 + y0, pl.ds(16 * z0, 16)]

    def scatter_z(p, block):
        for h in (0, 1):
            own = ft.at[block, :, pl.ds(128 * h, 128)]
            mine = lt.at[p, h, x0 * 4 + y0, pl.ds(16 * z0, 16)]
            pltpu.make_async_copy(own, mine, zsem.at[p]).start()
        for d in (1, 2, 3):
            pltpu.make_async_remote_copy(
                stage.at[block], chunk(p), zsend.at[p], zsem.at[p],
                device_id=(row, place(x0, y0, (z0 + d) % 4)), device_id_type=MESH,
            ).start()

    def half_copy(rows):
        return pltpu.make_async_remote_copy(
            rhs.at[0, rows], bh.at[0, rows], bsend.at[0], bsem.at[0],
            device_id=(other, real), device_id_type=MESH,
        )

    scatter_z(0, 0)
    for z in range(4):
        pltpu.make_async_remote_copy(
            stage.at[0], chunk(1), zsend.at[1], zsem.at[1],
            device_id=(other, place(x0, y0, z)), device_id_type=MESH,
        ).start()
    for p in range(2, AHEAD):
        scatter_z(p, p - 1)
    core_copy = pltpu.make_async_remote_copy(
        rhs.at[0], bh.at[1], bsend.at[1], bsem.at[1], device_id=(sibling, real), device_id_type=MESH
    )
    core_copy.start()
    last = pltpu.make_async_remote_copy(
        bh.at[0], bh.at[2], bsend.at[2], bsem.at[2], device_id=(sibling, real), device_id_type=MESH
    )

    def sibling_head(p):
        return pltpu.make_async_remote_copy(
            lt.at[p], lt.at[PIECES + p], xsend.at[p], xsem.at[p],
            device_id=(sibling, real), device_id_type=MESH,
        )

    def slab(p, h, a, b, half=None):
        x, y = ((x0 + a) % 4, (y0 + b) % 4) if h == 0 else ((x0 + b) % 4, (y0 + a) % 4)
        if half is None:
            return lt.at[p, h, x * 4 + y]
        return lt.at[p, h, x * 4 + y, pl.ds(32 * half, 32)]

    def target(h, first, step):
        if (h == 0) == first:
            return (row, place(x0 + step, y0, z0))
        return (row, place(x0, y0 + step, z0))

    def send(p, h, a, b, first, step, k, half=None):
        ref = slab(p, h, a, b, half)
        pltpu.make_async_remote_copy(
            ref, ref, ssem.at[p, h], rsem.at[p, h, k],
            device_id=target(h, first, step), device_id_type=MESH,
        ).start()

    def await_rows(p, h, k, slabs=1):
        ref = lt.at[p, h, pl.ds(0, slabs)]
        pltpu.make_async_copy(ref, ref, rsem.at[p, h, k]).wait()

    def phase1(p):
        ref = lt.at[p, :, 0]
        pltpu.make_async_copy(ref, ref, zsem.at[p]).wait()
        for h in (0, 1):
            send(p, h, 0, 0, True, 1, 1)
            send(p, h, 0, 0, True, 3, 2)
            send(p, h, 0, 0, False, 1, 4)
            send(p, h, 0, 0, False, 3, 5)

    def phase2(p):
        for h in (0, 1):
            await_rows(p, h, 1)
            send(p, h, 3, 0, True, 1, 3, 0)
            send(p, h, 3, 0, False, 1, 7)
            send(p, h, 3, 0, False, 3, 8)
        for h in (0, 1):
            await_rows(p, h, 2)
            send(p, h, 1, 0, True, 3, 3, 1)
            send(p, h, 1, 0, False, 1, 7)
            send(p, h, 1, 0, False, 3, 8)
        for h in (0, 1):
            await_rows(p, h, 4)
            send(p, h, 0, 3, False, 1, 6, 0)
            await_rows(p, h, 5)
            send(p, h, 0, 1, False, 3, 6, 1)

    def phase3(p):
        for h in (0, 1):
            await_rows(p, h, 3)
            send(p, h, 2, 0, False, 1, 10)
            send(p, h, 2, 0, False, 3, 11)
        for h in (0, 1):
            await_rows(p, h, 7, 2)
            send(p, h, 3, 3, False, 1, 9, 0)
            send(p, h, 1, 3, False, 1, 9, 0)
            await_rows(p, h, 8, 2)
            send(p, h, 3, 1, False, 3, 9, 1)
            send(p, h, 1, 1, False, 3, 9, 1)

    def phase4(p):
        for h in (0, 1):
            await_rows(p, h, 10)
            send(p, h, 2, 3, False, 1, 12, 0)
            await_rows(p, h, 11)
            send(p, h, 2, 1, False, 3, 12, 1)

    def finish(p):
        for h in (0, 1):
            await_rows(p, h, 6)
            await_rows(p, h, 9, 2)
            await_rows(p, h, 12)

    def slot_of(k):
        away, side = (k // 2 + zh) % 2, (k % 2 + core) % 2
        return away + PIECES * side, away + side + 3 * (1 - away) * (1 - side) - away * (1 - side)

    def diagonal(slot, k, h):
        return lt[slot, h, pl.ds(4 * k + 2 * h, 2)].reshape(128, 128)

    def invert_pair(slots, rows):
        which = [(s, k, h) for s, k in zip(slots, rows) for h in (0, 1)]
        for (_, k, h), x in zip(which, invert([diagonal(*w) for w in which])):
            xinv[k, h] = x

    def write(b):
        return pltpu.make_async_copy(work.at[b], out.at[b], outsem.at[b])

    def solve():
        for k in range(4):
            slot, index = slot_of(k)
            for h in (0, 1):
                at = 256 * k + 128 * h
                value = bh[index, pl.ds(128 * h, 128), :]
                if at:
                    part = lt[slot, h, pl.ds(0, at // 64)].reshape(at, 128)
                    value = value - product(part, yh[0:at, :], yl[0:at, :])
                answer = dot_t(xinv[k, h], value, HI)
                y[at : at + 128, :] = answer
                high, low = split(answer)
                yh[at : at + 128, :] = high
                yl[at : at + 128, :] = low
        work[0] = y[pl.ds(pl.multiple_of(row * 256, 256), 256), :]

    def trail(p):
        for h in (0, 1):
            rows = pl.ds(128 * h, 128)
            update = product(lt[p, h].reshape(1024, 128), yh[...], yl[...])
            work[p - 1, rows, :] = work[p - 1, rows, :] - update
        write(p - 1).start()

    @pl.loop(0, PIECES + 5)
    def _(t):
        pl.when(t + AHEAD < PIECES)(lambda: scatter_z(t + AHEAD, t + AHEAD - 1))
        pl.when(t < PIECES)(lambda: phase1(t))
        pl.when((t >= 2) & (t < PIECES + 2))(lambda: phase2(t - 2))
        pl.when((t >= 3) & (t < PIECES + 3))(lambda: phase3(t - 3))
        pl.when((t >= 4) & (t < PIECES + 4))(lambda: phase4(t - 4))
        pl.when(t >= 5)(lambda: finish(t - 5))

        pl.when((t >= RIGHT_FROM) & (t < RIGHT_FROM + 4))(
            lambda: half_copy(pl.ds(64 * (t - RIGHT_FROM), 64)).start()
        )

        @pl.when(t == RIGHT_BY)
        def _():
            half_copy(pl.ds(0, 256)).wait()
            last.start()

        @pl.when(t == 6)
        def _():
            for p in (0, 1):
                sibling_head(p).start()

        @pl.when(t == INVERT_OWN)
        def _():
            invert_pair((0, 1), (row, other))

        @pl.when(t == INVERT_SIBLING)
        def _():
            for p in (0, 1):
                sibling_head(p).wait()
            invert_pair((PIECES, PIECES + 1), (sibling, (1 - zh) * 2 + 1 - core))

        @pl.when(t == SOLVE)
        def _():
            core_copy.wait()
            last.wait()
            pltpu.make_async_copy(rhs, work, insem.at[0]).wait()
            pltpu.make_async_copy(rhs.at[0], bh.at[3], insem.at[1]).wait()
            solve()
            write(0).start()

        late = t // (SOLVE + 3)

        @pl.loop(0, 3)
        def _(q):
            p = (1 - late) * (2 + 3 * (t - SOLVE - 1) + q) + late * (t - 5)
            pl.when((t > SOLVE) & (late * q == 0) & (p <= t - 5))(lambda: trail(p))

    @pl.loop(0, PIECES)
    def _(p):
        part = lt.at[p, :, 0, pl.ds(0, 48)]
        pltpu.make_async_copy(part, part, zsend.at[p]).wait()
        for h in (0, 1):
            part = lt.at[p, h, pl.ds(0, 15)]
            pltpu.make_async_copy(part, part, ssem.at[p, h]).wait()

    part = lt.at[1, :, 0, pl.ds(0, 16)]
    pltpu.make_async_copy(part, part, zsend.at[1]).wait()

    @pl.loop(0, 10)
    def _(b):
        write(b).wait()


def substitute(ft, rhs):
    dma = pltpu.SemaphoreType.DMA
    anywhere = pl.BlockSpec(memory_space=pl.ANY)
    return pl.pallas_call(
        kernel,
        out_shape=jax.ShapeDtypeStruct((10, 256, 512), jnp.float32),
        in_specs=[anywhere, anywhere],
        out_specs=anywhere,
        scratch_shapes=[
            pltpu.VMEM((SLOTS, 2, 16, 64, 128), jnp.float32),
            pltpu.VMEM((10, 2, 16, 128), jnp.float32),
            pltpu.VMEM((4, 256, 512), jnp.float32),
            pltpu.VMEM((10, 256, 512), jnp.float32),
            pltpu.VMEM((4, 2, 128, 128), jnp.float32),
            pltpu.VMEM((1024, 512), jnp.float32),
            pltpu.VMEM((1024, 512), jnp.bfloat16),
            pltpu.VMEM((1024, 512), jnp.bfloat16),
            dma((PIECES, 2, 13)), dma((PIECES,)), dma((PIECES,)), dma((PIECES, 2)), dma((2,)),
            dma((3,)), dma((3,)), dma((2,)), dma((2,)), dma((2,)), dma((10,)),
        ],
        compiler_params=pltpu.CompilerParams(
            collective_id=0, has_side_effects=True, vmem_limit_bytes=60 * 1024 * 1024
        ),
        name="substitute",
    )(ft, rhs)


def body(right_sides, factor):
    return substitute(jnp.swapaxes(factor[:, 0], 1, 2), right_sides[:, 0])[:, None]


def solution(mesh):
    placed = (P(None, "row", None, "real"), P(None, "row", None, "real"))
    return jax.shard_map(
        body, mesh=mesh, in_specs=placed, out_specs=P(None, "row", None, "real"), check_vma=False
    )
```

time: 710 us -> 93.4 us (0.13)
  waiting for transfers between devices: 492 us -> 0 us
  Pallas kernels: 0 us -> 87.9 us
  other arithmetic: 85.1 us -> 0 us
  local copies, waits for them, and re-layouts: 70.3 us -> 5.42 us
  matrix products: 46.4 us -> 0 us
  between operations: 13.5 us -> 0.01 us
    all_gather x1 -> x0, waiting for transfers between devices: 350 us -> none  [body(): gathered = lax.all_gather(factor, 'real', axis=3, tiled=True)[:, 0]]
    psum x4 -> x0, waiting for transfers between devices: 141 us -> none  [broadcast(): return lax.psum(kept, axis)]
    pallas_call x0 -> x1, Pallas kernels: none -> 87.9 us  [substitute(): pl.pallas_call(kernel, out_shape=jax.ShapeDtypeStruct((10, 256, 512), jnp...]
    another operation x6 -> x0, other arithmetic: 78.8 us -> none  [forward_chain(): lax.linalg.triangular_solve(columns, current, left_side=True, lower=True)]
    dot_general x5 -> x0, matrix products: 41.3 us -> none  [the longest x1 32.6 us: body(): jnp.einsum('bpw,wc->bpc', gathered[1:], window_solved, precision=lax.Prec...]
    unnamed x10 -> x1, local copies, waits for them, and re-layouts: 29.7 us -> 5.42 us
    another operation x44 -> x0, local copies, waits for them, and re-layouts: 16.5 us -> none  [forward_chain(): lax.linalg.triangular_solve(columns, current, left_side=True, lower=True)]
    slice x3 -> x0, local copies, waits for them, and re-layouts: 15.8 us -> none  [the longest x1 8.87 us: body(): gathered[1:]]
  transfers between devices with their start and end apart: 5 -> 0, of which waited for: 5 -> 0; matrix products, arithmetic and copies ran while one was open for 16% -> 0% of each run, Pallas kernels for 0% -> 0%
where the time goes in v2:
time: 93.4 us; the launch traced here: 93.3 us
  Pallas kernels  87.9 us (94%)
  local copies, waits for them, and re-layouts  5.42 us (6%)
    pallas_call x1, Pallas kernels, substitute(): pl.pallas_call(kernel, out_shape=jax.ShapeDtypeStruct((10, 256, 512), jnp...  87.9 us
    unnamed x1, local copies, waits for them, and re-layouts  5.42 us

profile of v2, /device:TPU:2, one launch (start us, length us, event | category | flops | bytes accessed | tf_op | source)
XLA Modules:
  0.0 93.3 jit_solution(3234847730852907589)
XLA Ops:
  0.0 87.9 %substitute.1 = f32[10,256,512]{2,1,0:T(8,128)} custom-call(f32[10,16,256]{2,1,0:T(8,128)} %bitcast.9, f32[10,256,512]{2,1,0:T(8,128)} %bitcast.8), custom_call_target="tpu_custom_call" | custom-call | tf_op jit(solution)/shard_map/substitute/pallas_call | solution.py:305
  87.9 5.4 %copy.5 = f32[10,1,256,512]{3,2,1,0:T(8,128)} copy(f32[10,1,256,512]{3,2,1,0:T(8,128)} %bitcast.7) | data formatting | bytes 10485760

commit v3 on v2

--- a/solution.py
+++ b/solution.py
@@ -10,7 +10,7 @@
 SLOTS = 13
 AHEAD = 4
 RIGHT_FROM, RIGHT_BY = 4, 9
-INVERT_OWN, INVERT_SIBLING, SOLVE = 7, 8, 10
+INVERT_OWN, INVERT_SIBLING, SOLVE = 7, 9, 10
 HI = lax.Precision.HIGHEST
 
 
@@ -51,8 +51,8 @@
 
 
 def kernel(
-    ft, rhs, out, lt, stage, bh, work, xinv, y, yh, yl,
-    rsem, zsem, zsend, ssem, stsem, bsem, bsend, xsem, xsend, insem, outsem,
+    ft, rhs, work, lt, stage, bh, xinv, y, yh, yl,
+    rsem, zsem, zsend, ssem, stsem, bsem, bsend, xsem, xsend, insem,
 ):
     row = lax.axis_index("row")
     real = lax.axis_index("real")
@@ -208,9 +208,6 @@
         for (_, k, h), x in zip(which, invert([diagonal(*w) for w in which])):
             xinv[k, h] = x
 
-    def write(b):
-        return pltpu.make_async_copy(work.at[b], out.at[b], outsem.at[b])
-
     def solve():
         for k in range(4):
             slot, index = slot_of(k)
@@ -232,7 +229,6 @@
             rows = pl.ds(128 * h, 128)
             update = product(lt[p, h].reshape(1024, 128), yh[...], yl[...])
             work[p - 1, rows, :] = work[p - 1, rows, :] - update
-        write(p - 1).start()
 
     @pl.loop(0, PIECES + 5)
     def _(t):
@@ -274,7 +270,6 @@
             pltpu.make_async_copy(rhs, work, insem.at[0]).wait()
             pltpu.make_async_copy(rhs.at[0], bh.at[3], insem.at[1]).wait()
             solve()
-            write(0).start()
 
         late = t // (SOLVE + 3)
 
@@ -294,40 +289,37 @@
     part = lt.at[1, :, 0, pl.ds(0, 16)]
     pltpu.make_async_copy(part, part, zsend.at[1]).wait()
 
-    @pl.loop(0, 10)
-    def _(b):
-        write(b).wait()
-
 
 def substitute(ft, rhs):
     dma = pltpu.SemaphoreType.DMA
-    anywhere = pl.BlockSpec(memory_space=pl.ANY)
+    hbm = pl.BlockSpec(memory_space=pltpu.HBM)
     return pl.pallas_call(
         kernel,
-        out_shape=jax.ShapeDtypeStruct((10, 256, 512), jnp.float32),
-        in_specs=[anywhere, anywhere],
-        out_specs=anywhere,
+        out_shape=pltpu.VMEM((10, 256, 512), jnp.float32),
+        in_specs=[hbm, hbm],
+        out_specs=pl.BlockSpec(memory_space=pltpu.VMEM),
         scratch_shapes=[
             pltpu.VMEM((SLOTS, 2, 16, 64, 128), jnp.float32),
             pltpu.VMEM((10, 2, 16, 128), jnp.float32),
             pltpu.VMEM((4, 256, 512), jnp.float32),
-            pltpu.VMEM((10, 256, 512), jnp.float32),
             pltpu.VMEM((4, 2, 128, 128), jnp.float32),
             pltpu.VMEM((1024, 512), jnp.float32),
             pltpu.VMEM((1024, 512), jnp.bfloat16),
             pltpu.VMEM((1024, 512), jnp.bfloat16),
             dma((PIECES, 2, 13)), dma((PIECES,)), dma((PIECES,)), dma((PIECES, 2)), dma((2,)),
-            dma((3,)), dma((3,)), dma((2,)), dma((2,)), dma((2,)), dma((10,)),
+            dma((3,)), dma((3,)), dma((2,)), dma((2,)), dma((2,)),
         ],
         compiler_params=pltpu.CompilerParams(
-            collective_id=0, has_side_effects=True, vmem_limit_bytes=60 * 1024 * 1024
+            collective_id=0, has_side_effects=True, vmem_limit_bytes=36 * 1024 * 1024
         ),
         name="substitute",
     )(ft, rhs)
 
 
 def body(right_sides, factor):
-    return substitute(jnp.swapaxes(factor[:, 0], 1, 2), right_sides[:, 0])[:, None]
+    ft = pltpu.with_memory_space_constraint(jnp.swapaxes(factor[:, 0], 1, 2), pltpu.HBM)
+    rhs = pltpu.with_memory_space_constraint(right_sides[:, 0], pltpu.HBM)
+    return substitute(ft, rhs)[:, None]
 
 
 def solution(mesh):

time: 93.4 us -> 88.7 us (0.950); the launches traced: 93.3 us -> 87.5 us
  local copies, waits for them, and re-layouts: 5.42 us -> 2.36 us
  Pallas kernels: 87.9 us -> 85.1 us
    unnamed x1, local copies, waits for them, and re-layouts: 5.42 us -> 2.36 us
    pallas_call x1, Pallas kernels: 87.9 us -> 85.1 us  [substitute(): pl.pallas_call(kernel, out_shape=pltpu.VMEM((10, 256, 512), jnp.float32),...]
where the time goes in v3:
time: 88.7 us; the launch traced here: 87.5 us
  Pallas kernels  85.1 us (96%)
  local copies, waits for them, and re-layouts  2.36 us (3%)
    pallas_call x1, Pallas kernels, substitute(): pl.pallas_call(kernel, out_shape=pltpu.VMEM((10, 256, 512), jnp.float32),...  85.1 us
    unnamed x1, local copies, waits for them, and re-layouts  2.36 us

profile of v3, /device:TPU:2, one launch (start us, length us, event | category | flops | bytes accessed | tf_op | source)
XLA Modules:
  0.0 87.5 jit_solution(13869463311622151557)
XLA Ops:
  0.0 85.1 %substitute.1 = f32[10,256,512]{2,1,0:T(8,128)S(1)} custom-call(f32[10,16,256]{2,1,0:T(8,128)} %bitcast.9, f32[10,256,512]{2,1,0:T(8,128)} %bitcast.8), custom_call_target="tpu_custom_call" | custom-call | tf_op jit(solution)/shard_map/substitute/pallas_call | solution.py:296
  85.1 2.4 %copy.5 = f32[10,1,256,512]{3,2,1,0:T(8,128)} copy(f32[10,1,256,512]{3,2,1,0:T(8,128)S(1)} %bitcast.7) | data formatting | bytes 10485760

commit v4 on v3

--- a/solution.py
+++ b/solution.py
@@ -10,7 +10,7 @@
 SLOTS = 13
 AHEAD = 4
 RIGHT_FROM, RIGHT_BY = 4, 9
-INVERT_OWN, INVERT_SIBLING, SOLVE = 7, 9, 10
+INVERT_OWN, INVERT_SIBLING, SOLVE = 6, 8, 10
 HI = lax.Precision.HIGHEST
 
 

time: 88.7 us -> 88.5 us (level)
  no operation moved by 1% of the time
where the time goes in v4:
time: 88.5 us; the launch traced here: 88.1 us
  Pallas kernels  85.8 us (97%)
  local copies, waits for them, and re-layouts  2.36 us (3%)
    pallas_call x1, Pallas kernels, substitute(): pl.pallas_call(kernel, out_shape=pltpu.VMEM((10, 256, 512), jnp.float32),...  85.8 us
    unnamed x1, local copies, waits for them, and re-layouts  2.36 us

profile of v4, /device:TPU:2, one launch (start us, length us, event | category | flops | bytes accessed | tf_op | source)
XLA Modules:
  0.0 88.1 jit_solution(17594400420907024469)
XLA Ops:
  0.0 85.8 %substitute.1 = f32[10,256,512]{2,1,0:T(8,128)S(1)} custom-call(f32[10,16,256]{2,1,0:T(8,128)} %bitcast.9, f32[10,256,512]{2,1,0:T(8,128)} %bitcast.8), custom_call_target="tpu_custom_call" | custom-call | tf_op jit(solution)/shard_map/substitute/pallas_call | solution.py:296
  85.8 2.4 %copy.5 = f32[10,1,256,512]{3,2,1,0:T(8,128)} copy(f32[10,1,256,512]{3,2,1,0:T(8,128)S(1)} %bitcast.7) | data formatting | bytes 10485760

commit v5 on v4

--- a/solution.py
+++ b/solution.py
@@ -9,7 +9,7 @@
 PIECES = 11
 SLOTS = 13
 AHEAD = 4
-RIGHT_FROM, RIGHT_BY = 4, 9
+RIGHT_AT, RIGHT_BY = (2, 4, 6, 7), 9
 INVERT_OWN, INVERT_SIBLING, SOLVE = 6, 8, 10
 HI = lax.Precision.HIGHEST
 
@@ -52,7 +52,7 @@
 
 def kernel(
     ft, rhs, work, lt, stage, bh, xinv, y, yh, yl,
-    rsem, zsem, zsend, ssem, stsem, bsem, bsend, xsem, xsend, insem,
+    rsem, zsem, zsend, ssem, stsem, bsem, bsend, xsem, xsend, insem, relay, rsend, rrecv,
 ):
     row = lax.axis_index("row")
     real = lax.axis_index("real")
@@ -94,10 +94,14 @@
                 device_id=(row, place(x0, y0, (z0 + d) % 4)), device_id_type=MESH,
             ).start()
 
-    def half_copy(rows):
+    def pass_on(way, step):
+        rows = pl.ds(128 * way, 128)
+        chip = (zh * 4 + z0 + (1, 7)[way]) % 8
+        source = rhs.at[0, rows] if step == 0 else relay.at[way, step - 1]
+        into = bh.at[0, rows] if step == 3 else relay.at[way, step]
         return pltpu.make_async_remote_copy(
-            rhs.at[0, rows], bh.at[0, rows], bsend.at[0], bsem.at[0],
-            device_id=(other, real), device_id_type=MESH,
+            source, into, rsend.at[way, step], rrecv.at[way, step],
+            device_id=(chip // 4 * 2 + core, place(x0, y0, chip % 4)), device_id_type=MESH,
         )
 
     scatter_z(0, 0)
@@ -239,13 +243,19 @@
         pl.when((t >= 4) & (t < PIECES + 4))(lambda: phase4(t - 4))
         pl.when(t >= 5)(lambda: finish(t - 5))
 
-        pl.when((t >= RIGHT_FROM) & (t < RIGHT_FROM + 4))(
-            lambda: half_copy(pl.ds(64 * (t - RIGHT_FROM), 64)).start()
-        )
+        for step, when in enumerate(RIGHT_AT):
+
+            @pl.when(t == when)
+            def _(step=step):
+                for way in (0, 1):
+                    if step:
+                        pass_on(way, step - 1).wait_recv()
+                    pass_on(way, step).start()
 
         @pl.when(t == RIGHT_BY)
         def _():
-            half_copy(pl.ds(0, 256)).wait()
+            for way in (0, 1):
+                pass_on(way, 3).wait_recv()
             last.start()
 
         @pl.when(t == 6)
@@ -277,6 +287,10 @@
         def _(q):
             p = (1 - late) * (2 + 3 * (t - SOLVE - 1) + q) + late * (t - 5)
             pl.when((t > SOLVE) & (late * q == 0) & (p <= t - 5))(lambda: trail(p))
+
+    for way in (0, 1):
+        for step in range(4):
+            pass_on(way, step).wait_send()
 
     @pl.loop(0, PIECES)
     def _(p):
@@ -308,6 +322,7 @@
             pltpu.VMEM((1024, 512), jnp.bfloat16),
             dma((PIECES, 2, 13)), dma((PIECES,)), dma((PIECES,)), dma((PIECES, 2)), dma((2,)),
             dma((3,)), dma((3,)), dma((2,)), dma((2,)), dma((2,)),
+            pltpu.VMEM((2, 3, 128, 512), jnp.float32), dma((2, 4)), dma((2, 4)),
         ],
         compiler_params=pltpu.CompilerParams(
             collective_id=0, has_side_effects=True, vmem_limit_bytes=36 * 1024 * 1024

time: 88.5 us -> 89.5 us (1.011)
  Pallas kernels: 85.8 us -> 87 us
    pallas_call x1, Pallas kernels: 85.8 us -> 87 us  [substitute(): pl.pallas_call(kernel, out_shape=pltpu.VMEM((10, 256, 512), jnp.float32),...]
where the time goes in v5:
time: 89.5 us; the launch traced here: 89.4 us
  Pallas kernels  87 us (97%)
  local copies, waits for them, and re-layouts  2.36 us (3%)
    pallas_call x1, Pallas kernels, substitute(): pl.pallas_call(kernel, out_shape=pltpu.VMEM((10, 256, 512), jnp.float32),...  87 us
    unnamed x1, local copies, waits for them, and re-layouts  2.36 us

profile of v5, /device:TPU:2, one launch (start us, length us, event | category | flops | bytes accessed | tf_op | source)
XLA Modules:
  0.0 89.4 jit_solution(1786693661533593030)
XLA Ops:
  0.0 87.0 %substitute.1 = f32[10,256,512]{2,1,0:T(8,128)S(1)} custom-call(f32[10,16,256]{2,1,0:T(8,128)} %bitcast.9, f32[10,256,512]{2,1,0:T(8,128)} %bitcast.8), custom_call_target="tpu_custom_call" | custom-call | tf_op jit(solution)/shard_map/substitute/pallas_call | solution.py:310
  87.1 2.4 %copy.5 = f32[10,1,256,512]{3,2,1,0:T(8,128)} copy(f32[10,1,256,512]{3,2,1,0:T(8,128)S(1)} %bitcast.7) | data formatting | bytes 10485760
